TPU v7x, 128 devices: a whole 4x4x4 slice. The times are simulated.
128 devices in a mesh: shard: 32 (over y, z_hi, x), tensor: 4 (over z_lo, core).
Axes of the slice: x: 4, y: 4, z: 4 (z_hi: 2, z_lo: 2; z = z_hi * 2 + z_lo), core: 2. Of those that a mesh axis runs over, the one named last changes fastest.
Arguments:
- acts: bfloat16 [32768, 768], P('shard', 'tensor')
- out_grads: bfloat16 [2, 32768, 768], P(None, 'shard', 'tensor')
- sampled_rows: int32 [2, 262144], P(None, 'shard'), may hold values from 0 to 1023
- proj_grad: float32 [768, 768], P(('shard', 'tensor')), may hold values from -600 to 600
- proj_momentum: float32 [768, 768], P(('shard', 'tensor')), may hold values from -6 to 6
- embed_grad: float32 [49152, 768], P(('shard', 'tensor')), may hold values from -36 to 36
- embed_momentum: float32 [49152, 768], P(('shard', 'tensor')), may hold values from -6 to 6
- token_counts: int32 [49152], P(('shard', 'tensor')), may hold values from 0 to 99
Outputs:
- proj_momentum_new: float32 [768, 768], P(('shard', 'tensor'))
- embed_momentum_new: float32 [49152, 768], P(('shard', 'tensor'))
Inputs may be any that keep to these rules, and one draw needn't show every extreme that they name: `sampled_rows`: entry j of a row picks token (j // 8192) * 1024 + value, one of the 1024 tokens of its index of shard; repeats are allowed.
All inputs are finite; a program needn't handle non-finite values.
Results may differ from a plain program's by a relative error of at most 0.0003.
Values may be sent and summed in bfloat16 or wider, within the bound.
No kernel may reach another device: no remote copies, remote signals or barrier semaphores. Data moves between devices by JAX's collectives and lax.ppermute only.
A program may use at most 128 MiB of HBM per device.

v0:
```python
import jax
import jax.numpy as jnp
from jax import lax
from jax.sharding import PartitionSpec as P

D = 768
VOCAB = 49152
SAMPLE = 2048
NS_ITERS = 3
momentum_decay = 0.9
damping_root = 0.5
count_scale = 64.0
highest = lax.Precision.HIGHEST


def per_device(
    acts,
    out_grads,
    sampled_rows,
    proj_grad,
    proj_momentum,
    embed_grad,
    embed_momentum,
    token_counts,
):
    n_shard = lax.axis_size("shard")
    n_tensor = lax.axis_size("tensor")
    devices_all = n_shard * n_tensor
    flat_index = lax.axis_index("shard") * n_tensor + lax.axis_index("tensor")
    width = D
    row_count = width // devices_all
    sample_total = SAMPLE * devices_all
    picked = jnp.stack(
        [
            jnp.take(acts, sampled_rows[0], axis=0),
            jnp.take(out_grads[0], sampled_rows[0], axis=0),
            jnp.take(out_grads[1], sampled_rows[1], axis=0),
        ]
    )
    sampled = lax.all_to_all(picked, "tensor", split_axis=1, concat_axis=2, tiled=True)
    trace_part = jnp.sum(jnp.square(sampled.astype(jnp.float32)), axis=(1, 2))
    factor_rows = (
        lax.psum_scatter(
            jnp.einsum("fsd,fse->dfe", sampled, sampled, preferred_element_type=jnp.float32),
            ("shard", "tensor"),
            scatter_dimension=0,
            tiled=True,
        )
        / sample_total
    )
    frob_part = jnp.sum(factor_rows * factor_rows, axis=(0, 2))
    count_part = jnp.sum(token_counts).astype(jnp.float32)
    frob_total, trace_total, count_total = lax.psum(
        (frob_part, trace_part, count_part), ("shard", "tensor")
    )
    traces = trace_total / sample_total
    ratio = jnp.sqrt(traces[0] / traces[1])
    embed_ratio = jnp.sqrt(count_total / count_scale / VOCAB / (traces[2] / width))
    shifts = jnp.stack([damping_root * ratio, damping_root / ratio, damping_root / embed_ratio])
    norm_sq = frob_total + 2.0 * shifts * traces + width * shifts * shifts
    start_scale = 1.0 / jnp.sqrt(norm_sq)
    row_ids = flat_index * row_count + jnp.arange(row_count, dtype=jnp.int32)
    eye_rows = (jnp.arange(width, dtype=jnp.int32)[None, :] == row_ids[:, None]).astype(
        jnp.float32
    )[:, None, :]
    damped = factor_rows + shifts[None, :, None] * eye_rows
    rows_now = (
        2.0 * start_scale[None, :, None] * eye_rows
        - (start_scale * start_scale)[None, :, None] * damped
    )
    for iteration in range(NS_ITERS):
        inverses = lax.all_gather(rows_now, ("shard", "tensor"), axis=0, tiled=True)
        if iteration < NS_ITERS - 1:
            product = jnp.einsum("rfk,kfj->rfj", damped, inverses, precision=highest)
            rows_now = 2.0 * rows_now - jnp.einsum(
                "rfk,kfj->rfj", product, inverses, precision=highest
            )
    g_inverse = inverses[:, 1, :]
    e_inverse = inverses[:, 2, :]
    a_rows = lax.dynamic_slice_in_dim(inverses[:, 0, :], flat_index * row_count, row_count, 0)
    mixed_rows = jnp.dot(proj_grad, g_inverse, precision=highest)
    update = jnp.dot(
        a_rows,
        lax.all_gather(mixed_rows, ("shard", "tensor"), axis=0, tiled=True),
        precision=highest,
    )
    row_scale = token_counts.astype(jnp.float32) / count_scale + damping_root * embed_ratio
    embed_update = jnp.dot(embed_grad, e_inverse, precision=highest) / row_scale[:, None]
    return (momentum_decay * proj_momentum + update, momentum_decay * embed_momentum + embed_update)


def solution(mesh):
    return jax.shard_map(
        per_device,
        mesh=mesh,
        in_specs=(
            P("shard", "tensor"),
            P(None, "shard", "tensor"),
            P(None, "shard"),
            P(("shard", "tensor"), None),
            P(("shard", "tensor"), None),
            P(("shard", "tensor"), None),
            P(("shard", "tensor"), None),
            P(("shard", "tensor")),
        ),
        out_specs=(P(("shard", "tensor"), None), P(("shard", "tensor"), None)),
        check_vma=False,
    )
```

profile of v0, /device:TPU:1, one launch (start us, length us, event | category | flops | bytes accessed | tf_op | source)
XLA Modules:
  0.0 1483.3 jit_solution(11976387362760375360)
XLA Ops:
  8.3 1.2 copy.48
  9.5 1.2 fusion.61
  11.1 32.9 %gather_fusion.1 = bf16[8192,192]{1,0:T(8,128)(2,1)} fusion(bf16[1024,192]{1,0:T(8,128)(2,1)S(1)} %bitcast.65, s32[8192]{0:T(1024)S(1)} %fusion.50), kind=kCustom, calls=%fused_computation.1.clone | custom fusion | bytes 6324224 | tf_op jit(solution)/shard_map/jit(_take)/gather | solution.py:36
  44.0 32.9 %gather_fusion = bf16[8192,192]{1,0:T(8,128)(2,1)} fusion(bf16[1024,192]{1,0:T(8,128)(2,1)S(1)} %copy.48, s32[8192]{0:T(1024)S(1)} %fusion.50), kind=kCustom, calls=%fused_computation.clone | custom fusion | bytes 6324224 | tf_op jit(solution)/shard_map/jit(_take)/gather | solution.py:35
  76.9 32.9 %gather_fusion.2 = bf16[8192,192]{1,0:T(8,128)(2,1)} fusion(bf16[1024,192]{1,0:T(8,128)(2,1)S(1)} %bitcast.64, s32[8192]{0:T(1024)S(1)} %fusion.51), kind=kCustom, calls=%fused_computation.2.clone | custom fusion | bytes 6324224 | tf_op jit(solution)/shard_map/jit(_take)/gather | solution.py:37
  109.9 6.8 select_bitcast_fusion
  116.7 4.3 select_bitcast_fusion.2
  121.0 6.2 pad_maximum_fusion
  127.2 17.9 %copy.51 = bf16[3,8192,192]{2,0,1:T(4,128)(2,1)S(1)} copy(bf16[3,8192,192]{2,1,0:T(8,128)(2,1)} %pad_maximum_fusion) | data formatting | bytes 18874368 | tf_op jit(solution)/shard_map/stack | solution.py:33
  145.1 187.7 %all_to_all.18 = bf16[3,8192,192]{2,0,1:T(4,128)(2,1)} all-to-all(bf16[3,8192,192]{2,0,1:T(4,128)(2,1)S(1)} %copy.51), channel_id=1, replica_groups=mesh['shard'=32,'tensor'=4] {'tensor'}, dimensions={1} | all-to-all | bytes 18874368 | tf_op jit(solution)/shard_map/all_to_all | solution.py:40
  332.8 24.3 %copy.53 = bf16[3,2048,4,192]{1,3,2,0:T(8,128)(2,1)} copy(bf16[3,2048,4,192]{3,0,1,2:T(4,128)(2,1)} %bitcast.66) | data formatting | bytes 18874368 | tf_op jit(solution)/shard_map/all_to_all | solution.py:40
  357.0 14.6 convolution_bitcast_fusion
  371.7 11.0 copy.55
  384.7 26.6 %copy.67 = bf16[3,4,2048,192]{2,1,3,0:T(4,128)(2,1)} copy(bf16[3,4,2048,192]{3,0,2,1:T(4,128)(2,1)} %bitcast.67) | data formatting | bytes 18874368 | tf_op jit(solution)/shard_map/all_to_all | solution.py:40
  411.2 10.6 multiply_reduce_fusion
  421.8 127.8 %all-reduce.4.cloned.1.call-done = f32[768,3,768]{2,1,0:T(4,128)} async-done(((f32[768,3,768]{2,1,0:T(4,128)}), f32[768,3,768]{2,1,0:T(4,128)}) %all-reduce.4.cloned.1.call-update) | async-done | bytes 7077904
  550.7 64.2 %all-reduce.1 = (f32[]{:T(128)}, f32[3]{0:T(128)S(1)}, f32[3]{0:T(128)S(1)}) all-reduce(f32[]{:T(128)S(6)} %convert_element_type.18, f32[3]{0:T(128)S(1)} %multiply_reduce_fusion, f32[3]{0:T(128)S(1)} %multiply_reduce_fusion.1), channel_id=1, replica_groups=mesh['shard'=32,'tensor'=4] {'shard','tensor'}, use_global_device_ids=true, to_apply=%region_6.8 | all-reduce | flops 7 | bytes 56 | tf_op jit(solution)/shard_map/psum | solution.py:53
  619.4 199.9 %all-gather.6.cloned.1.call-done = f32[768,3,768]{2,1,0:T(4,128)} async-done(((f32[6,3,768]{2,1,0:T(4,128)}), f32[768,3,768]{2,1,0:T(4,128)}) %all-gather.6.cloned.1.call-update) | async-done | bytes 7077904 | tf_op jit(solution)/shard_map/all_gather | solution.py:72
  819.3 7.9 fusion.29
  827.2 7.9 fusion.26
  836.1 201.5 %all-gather.8.cloned.1.call-done = f32[768,3,768]{2,1,0:T(4,128)} async-done(((f32[6,3,768]{2,1,0:T(4,128)}), f32[768,3,768]{2,1,0:T(4,128)}) %all-gather.8.cloned.1.call-update) | async-done | bytes 7077904 | tf_op jit(solution)/shard_map/all_gather | solution.py:72
  1037.6 7.9 fusion.38
  1045.5 7.9 fusion.35
  1054.4 201.6 %all-gather.10.cloned.1.call-done = f32[768,3,768]{2,1,0:T(4,128)} async-done(((f32[6,3,768]{2,1,0:T(4,128)}), f32[768,3,768]{2,1,0:T(4,128)}) %all-gather.10.cloned.1.call-update) | async-done | bytes 7077904 | tf_op jit(solution)/shard_map/all_gather | solution.py:72
  1256.0 16.8 %fusion.60 = (f32[768,1,768]{2,1,0:T(1,128)}, f32[768,1,768]{2,1,0:T(1,128)S(1)}, f32[768,1,768]{2,1,0:T(1,128)S(1)}) fusion(f32[768,3,768]{2,1,0:T(4,128)} %all-gather.10.cloned.1.call-done), kind=kLoop, calls=%fused_computation.66 | loop fusion | bytes 14155776 | tf_op jit(solution)/shard_map/slice | solution.py:79
  1272.8 2.7 fusion.41
  1275.5 2.7 copy.64
  1278.2 10.5 fusion.20
  1288.7 2.7 copy.65
  1291.9 179.2 %all-gather.12.cloned.1.call-done = f32[128,6,768]{2,1,0:T(8,128)} async-done(((f32[1,6,768]{2,1,0:T(8,128)}), f32[128,6,768]{2,1,0:T(8,128)}) %all-gather.12.cloned.1.call-update) | async-done | bytes 2359312 | tf_op jit(solution)/shard_map/all_gather | solution.py:84
  1471.1 2.7 reshape.75
  1473.8 2.6 convolution_add_fusion
  (40 shorter events, 8.2 us)
Async XLA Ops:
  7.2 1271.0 %copy-start = (f32[384,768]{1,0:T(8,128)S(1)}, f32[384,768]{1,0:T(8,128)}, u32[]{:S(2)}) copy-start(f32[384,768]{1,0:T(8,128)} %param.15) | copy-start | bytes 3538948
  7.2 542.4 %all-reduce.4.cloned.1.call-start = ((), (), s32[]{:S(2)}) async-start(), calls=%async_computation.5 | async-start | bytes 18874368
  109.9 6.8 copy-start.1
  109.9 6.9 copy-start.2
  382.7 0.7 copy-start.3
  382.7 436.6 %all-gather.6.cloned.1.call-start = ((), (), s32[]{:S(2)}) async-start(), calls=%async_computation.1 | async-start | bytes 9510912 | tf_op jit(solution)/shard_map/all_gather | solution.py:72
  619.2 418.4 %all-gather.8.cloned.1.call-start = ((), (), s32[]{:S(2)}) async-start(), calls=%async_computation.2 | async-start | bytes 9510912 | tf_op jit(solution)/shard_map/all_gather | solution.py:72
  835.8 420.2 %all-gather.10.cloned.1.call-start = ((), (), s32[]{:S(2)}) async-start(), calls=%async_computation.3 | async-start | bytes 9510912 | tf_op jit(solution)/shard_map/all_gather | solution.py:72
  1054.1 417.0 %all-gather.12.cloned.1.call-start = ((), (), s32[]{:S(2)}) async-start(), calls=%async_computation.4 | async-start | bytes 3170304 | tf_op jit(solution)/shard_map/all_gather | solution.py:84
Sparse Core Ops, SparseCore 0:
  382.8 166.7 all-reduce.3
  619.3 199.9 all-gather.5
  835.9 201.5 all-gather.7
  1054.2 201.7 all-gather.9
  1275.6 195.4 all-gather.11
where the time goes:
time: 1490 us; the launch traced here: 1480 us
  waiting for transfers between devices  910 us (61%)
  blocking collectives  252 us (17%)
  local copies, waits for them, and re-layouts  211 us (14%)
  matrix products  62.1 us (4%)
  other arithmetic  29 us (2%)
  between operations  17.8 us (1%)
    all_gather x3, waiting for transfers between devices, per_device(): inverses = lax.all_gather(rows_now, ('shard', 'tensor'), axis=0, tiled=True)  603 us
    all_to_all x1, blocking collectives, per_device(): lax.all_to_all(picked, 'tensor', split_axis=1, concat_axis=2, tiled=True)  188 us
    all_gather x1, waiting for transfers between devices, per_device(): lax.all_gather(mixed_rows, ('shard', 'tensor'), axis=0, tiled=True)  179 us
    unnamed x6, waiting for transfers between devices  128 us
    psum x1, blocking collectives, per_device(): lax.psum((frob_part, trace_part, count_part), ('shard', 'tensor'))  64.2 us
    all_to_all x2, local copies, waits for them, and re-layouts, per_device(): lax.all_to_all(picked, 'tensor', split_axis=1, concat_axis=2, tiled=True)  50.8 us
    gather x1, local copies, waits for them, and re-layouts, per_device(): jnp.take(out_grads[0], sampled_rows[0], axis=0)  32.9 us
    gather x1, local copies, waits for them, and re-layouts, per_device(): jnp.take(out_grads[1], sampled_rows[1], axis=0)  32.9 us
  transfers between devices with their start and end apart: 5, of which 5 were waited for; matrix products, arithmetic and copies ran while one was open for 4% of the time, Pallas kernels for 0%

commit v1 on v0

--- a/solution.py
+++ b/solution.py
@@ -37,7 +37,12 @@
             jnp.take(out_grads[1], sampled_rows[1], axis=0),
         ]
     )
-    sampled = lax.all_to_all(picked, "tensor", split_axis=1, concat_axis=2, tiled=True)
+    sampled = jnp.concatenate(
+        lax.all_to_all(
+            jnp.stack(jnp.split(picked, lax.axis_size("tensor"), axis=1)), "tensor", 0, 0
+        ),
+        axis=2,
+    )
     trace_part = jnp.sum(jnp.square(sampled.astype(jnp.float32)), axis=(1, 2))
     factor_rows = (
         lax.psum_scatter(

time: 1490 us -> 1400 us (0.940)
  blocking collectives: 252 us -> 177 us
  local copies, waits for them, and re-layouts: 211 us -> 168 us
  waiting for transfers between devices: 910 us -> 941 us
    all_to_all x1, blocking collectives: 188 us -> 113 us  [per_device(): lax.all_to_all(jnp.stack(jnp.split(picked, lax.axis_size('tensor'), axis=...]
    all_to_all x2 -> x1, local copies, waits for them, and re-layouts: 50.8 us -> 9.26 us  [per_device(): lax.all_to_all(jnp.stack(jnp.split(picked, lax.axis_size('tensor'), axis=...]
    unnamed x6, waiting for transfers between devices: 128 us -> 159 us
  transfers between devices with their start and end apart: 5 -> 5, of which waited for: 5 -> 5; matrix products, arithmetic and copies ran while one was open for 4% -> 2% of each run, Pallas kernels for 0% -> 0%
where the time goes in v1:
time: 1400 us; the launch traced here: 1390 us
  waiting for transfers between devices  941 us (67%)
  blocking collectives  177 us (13%)
  local copies, waits for them, and re-layouts  168 us (12%)
  matrix products  62.1 us (4%)
  other arithmetic  27.6 us (2%)
  between operations  17.6 us (1%)
    all_gather x3, waiting for transfers between devices, per_device(): inverses = lax.all_gather(rows_now, ('shard', 'tensor'), axis=0, tiled=True)  603 us
    all_gather x1, waiting for transfers between devices, per_device(): lax.all_gather(mixed_rows, ('shard', 'tensor'), axis=0, tiled=True)  179 us
    unnamed x6, waiting for transfers between devices  159 us
    all_to_all x1, blocking collectives, per_device(): lax.all_to_all(jnp.stack(jnp.split(picked, lax.axis_size('tensor'), axis=...  113 us
    psum x1, blocking collectives, per_device(): lax.psum((frob_part, trace_part, count_part), ('shard', 'tensor'))  64.2 us
    gather x1, local copies, waits for them, and re-layouts, per_device(): jnp.take(out_grads[0], sampled_rows[0], axis=0)  33.1 us
    gather x1, local copies, waits for them, and re-layouts, per_device(): jnp.take(out_grads[1], sampled_rows[1], axis=0)  33.1 us
    gather x1, local copies, waits for them, and re-layouts, per_device(): jnp.take(acts, sampled_rows[0], axis=0)  33.1 us
  transfers between devices with their start and end apart: 5, of which 5 were waited for; matrix products, arithmetic and copies ran while one was open for 2% of the time, Pallas kernels for 0%

profile of v1, /device:TPU:1, one launch (start us, length us, event | category | flops | bytes accessed | tf_op | source)
XLA Modules:
  0.0 1394.5 jit_solution(2369349266689683021)
XLA Ops:
  8.3 1.2 copy.32
  9.5 1.2 fusion.61
  11.1 33.1 %gather_fusion.1 = bf16[8192,192]{1,0:T(8,128)(2,1)} fusion(bf16[1024,192]{1,0:T(8,128)(2,1)S(1)} %bitcast.71, s32[8192]{0:T(1024)S(1)} %fusion.50), kind=kCustom, calls=%fused_computation.1.clone | custom fusion | bytes 6324224 | tf_op jit(solution)/shard_map/jit(_take)/gather | solution.py:36
  44.2 33.1 %gather_fusion = bf16[8192,192]{1,0:T(8,128)(2,1)} fusion(bf16[1024,192]{1,0:T(8,128)(2,1)S(1)} %copy.32, s32[8192]{0:T(1024)S(1)} %fusion.50), kind=kCustom, calls=%fused_computation.clone | custom fusion | bytes 6324224 | tf_op jit(solution)/shard_map/jit(_take)/gather | solution.py:35
  77.3 33.1 %gather_fusion.2 = bf16[8192,192]{1,0:T(8,128)(2,1)} fusion(bf16[1024,192]{1,0:T(8,128)(2,1)S(1)} %bitcast.70, s32[8192]{0:T(1024)S(1)} %fusion.51), kind=kCustom, calls=%fused_computation.2.clone | custom fusion | bytes 6324224 | tf_op jit(solution)/shard_map/jit(_take)/gather | solution.py:37
  110.4 6.8 select_bitcast_fusion
  117.2 4.3 select_bitcast_fusion.2
  121.5 2.9 pad_maximum_fusion
  125.6 6.5 pad_maximum_fusion.1
  132.0 14.9 %copy.35 = bf16[4,3,2048,192]{2,3,1,0:T(8,128)(2,1)} copy(bf16[4,3,2048,192]{3,2,1,0:T(8,128)(2,1)} %pad_maximum_fusion.1) | data formatting | bytes 18874368 | tf_op jit(solution)/shard_map/stack | solution.py:42
  146.9 112.6 %all_to_all.5 = bf16[4,3,2048,192]{2,3,1,0:T(8,128)(2,1)} all-to-all(bf16[4,3,2048,192]{2,3,1,0:T(8,128)(2,1)} %copy.35), channel_id=1, replica_groups=mesh['shard'=32,'tensor'=4] {'tensor'}, dimensions={0} | all-to-all | bytes 18874368 | tf_op jit(solution)/shard_map/all_to_all | solution.py:41
  259.5 9.3 copy.36
  268.8 14.7 %convolution_bitcast_fusion = f32[768,3,768]{0,2,1:T(8,128)} fusion(bf16[3,2048,768]{1,2,0:T(8,128)(2,1)} %bitcast.72), kind=kOutput, calls=%fused_computation.21 | convolution fusion | flops 7247757312 | bytes 16515072 | tf_op jit(solution)/shard_map/fsd,fse->dfe/dot_general | solution.py:49
  283.4 11.0 copy.38
  296.4 6.0 multiply_reduce_fusion
  302.4 158.7 %all-reduce.4.cloned.1.call-done = f32[768,3,768]{2,1,0:T(4,128)} async-done(((f32[768,3,768]{2,1,0:T(4,128)}), f32[768,3,768]{2,1,0:T(4,128)}) %all-reduce.4.cloned.1.call-update) | async-done | bytes 7077904
  462.2 64.2 %all-reduce.1 = (f32[]{:T(128)}, f32[3]{0:T(128)S(1)}, f32[3]{0:T(128)S(1)}) all-reduce(f32[]{:T(128)S(6)} %convert_element_type.18, f32[3]{0:T(128)S(1)} %multiply_reduce_fusion, f32[3]{0:T(128)S(1)} %multiply_reduce_fusion.1), channel_id=1, replica_groups=mesh['shard'=32,'tensor'=4] {'shard','tensor'}, use_global_device_ids=true, to_apply=%region_6.8 | all-reduce | flops 7 | bytes 56 | tf_op jit(solution)/shard_map/psum | solution.py:58
  530.6 200.1 %all-gather.6.cloned.1.call-done = f32[768,3,768]{2,1,0:T(4,128)} async-done(((f32[6,3,768]{2,1,0:T(4,128)}), f32[768,3,768]{2,1,0:T(4,128)}) %all-gather.6.cloned.1.call-update) | async-done | bytes 7077904 | tf_op jit(solution)/shard_map/all_gather | solution.py:77
  730.7 7.9 fusion.29
  738.6 7.9 fusion.26
  747.5 201.5 %all-gather.8.cloned.1.call-done = f32[768,3,768]{2,1,0:T(4,128)} async-done(((f32[6,3,768]{2,1,0:T(4,128)}), f32[768,3,768]{2,1,0:T(4,128)}) %all-gather.8.cloned.1.call-update) | async-done | bytes 7077904 | tf_op jit(solution)/shard_map/all_gather | solution.py:77
  949.0 7.9 fusion.38
  956.9 7.9 fusion.35
  965.8 201.6 %all-gather.10.cloned.1.call-done = f32[768,3,768]{2,1,0:T(4,128)} async-done(((f32[6,3,768]{2,1,0:T(4,128)}), f32[768,3,768]{2,1,0:T(4,128)}) %all-gather.10.cloned.1.call-update) | async-done | bytes 7077904 | tf_op jit(solution)/shard_map/all_gather | solution.py:77
  1167.4 16.8 %fusion.60 = (f32[768,1,768]{2,1,0:T(1,128)}, f32[768,1,768]{2,1,0:T(1,128)S(1)}, f32[768,1,768]{2,1,0:T(1,128)S(1)}) fusion(f32[768,3,768]{2,1,0:T(4,128)} %all-gather.10.cloned.1.call-done), kind=kLoop, calls=%fused_computation.71 | loop fusion | bytes 14155776 | tf_op jit(solution)/shard_map/slice | solution.py:84
  1184.2 2.7 fusion.41
  1186.9 2.7 copy.47
  1189.6 10.5 fusion.20
  1200.1 2.7 copy.48
  1203.4 179.2 %all-gather.12.cloned.1.call-done = f32[128,6,768]{2,1,0:T(8,128)} async-done(((f32[1,6,768]{2,1,0:T(8,128)}), f32[128,6,768]{2,1,0:T(8,128)}) %all-gather.12.cloned.1.call-update) | async-done | bytes 2359312 | tf_op jit(solution)/shard_map/all_gather | solution.py:89
  1382.5 2.7 reshape.83
  1385.2 2.6 convolution_add_fusion
  (41 shorter events, 9.0 us)
Async XLA Ops:
  7.2 1182.4 %copy-start = (f32[384,768]{1,0:T(8,128)S(1)}, f32[384,768]{1,0:T(8,128)}, u32[]{:S(2)}) copy-start(f32[384,768]{1,0:T(8,128)} %param.15) | copy-start | bytes 3538948
  7.2 453.9 %all-reduce.4.cloned.1.call-start = ((), (), s32[]{:S(2)}) async-start(), calls=%async_computation.5 | async-start | bytes 18874368
  110.4 6.8 copy-start.1
  110.4 6.9 copy-start.2
  294.4 0.7 copy-start.3
  294.4 436.2 %all-gather.6.cloned.1.call-start = ((), (), s32[]{:S(2)}) async-start(), calls=%async_computation.1 | async-start | bytes 9510912 | tf_op jit(solution)/shard_map/all_gather | solution.py:77
  530.6 418.4 %all-gather.8.cloned.1.call-start = ((), (), s32[]{:S(2)}) async-start(), calls=%async_computation.2 | async-start | bytes 9510912 | tf_op jit(solution)/shard_map/all_gather | solution.py:77
  747.2 420.2 %all-gather.10.cloned.1.call-start = ((), (), s32[]{:S(2)}) async-start(), calls=%async_computation.3 | async-start | bytes 9510912 | tf_op jit(solution)/shard_map/all_gather | solution.py:77
  965.5 417.0 %all-gather.12.cloned.1.call-start = ((), (), s32[]{:S(2)}) async-start(), calls=%async_computation.4 | async-start | bytes 3170304 | tf_op jit(solution)/shard_map/all_gather | solution.py:89
Sparse Core Ops, SparseCore 0:
  294.6 166.4 all-reduce.3
  530.7 199.9 all-gather.5
  747.4 201.5 all-gather.7
  965.6 201.7 all-gather.9
  1187.1 195.4 all-gather.11
